TPU v7x, 512 devices: a whole 4x4x16 slice. The times are simulated.
512 devices in a mesh: gx: 32 (over y, x, core), gy: 16 (over z).
Axes of the slice: x: 4, y: 4, z: 16, core: 2. Of those that a mesh axis runs over, the one named last changes fastest.
Arguments:
- basis: bfloat16 [16, 4, 512, 4096], P(None, None, 'gy', 'gx'), may hold values from -56 to 56
- mobility: bfloat16 [4, 512, 4096], P(None, 'gy', 'gx'), may hold values from 0.12 to 8.2
- accumulation: float32 [4, 512, 4096], P(None, 'gy', 'gx'), may hold values from 0.03 to 0.32
- residual: float32 [4, 512, 4096], P(None, 'gy', 'gx'), may hold values from -140 to 140
Outputs:
- correction: float32 [4, 512, 4096], P(None, 'gy', 'gx')
- coarse_solution: float32 [32, 16, 16], P('gx', 'gy')
All inputs are finite; a program needn't handle non-finite values.
Results may differ from a plain program's by a relative error of at most 0.0003.
Values may be sent and summed in bfloat16 or wider, within the bound.
A program may use at most 64 MiB of HBM per device.

v0:
```python
import jax
import jax.numpy as jnp
from jax import lax
from jax.sharding import PartitionSpec as P

K = 16
ITERS = 2


epsilon = 1e-06
vertical_ratio = 0.1


def with_halo(x, sides, width):
    for axis, dim in sides:
        peers, length = (lax.axis_size(axis), x.shape[dim])
        up = [(i, (i + 1) % peers) for i in range(peers - 1)]
        down = [(j, i) for i, j in up]
        last = lax.slice_in_dim(x, length - width, length, axis=dim)
        initial = lax.slice_in_dim(x, 0, width, axis=dim)
        before = lax.ppermute(last, axis, up)
        after = lax.ppermute(initial, axis, down)
        x = jnp.concatenate([before, x, after], axis=dim)
    return x


def harmonic(first, second):
    return 2.0 * first * second / (first + second)


def gram_sum(weighted, other):
    return jnp.einsum("kzyx,lzyx->kl", weighted, other, precision=lax.Precision.HIGHEST)


def face_blocks(padded_basis, padded_mobility, accumulation):
    interior = padded_basis[:, :, 1:-1, 1:-1]
    cell_mobility = padded_mobility[:, 1:-1, 1:-1]
    self_block = gram_sum(interior * accumulation, interior)
    conduct_x = harmonic(cell_mobility[:, :, :-1], cell_mobility[:, :, 1:])
    change_x = interior[:, :, :, 1:] - interior[:, :, :, :-1]
    self_block = self_block + gram_sum(change_x * conduct_x, change_x)
    conduct_y = harmonic(cell_mobility[:, :-1, :], cell_mobility[:, 1:, :])
    change_y = interior[:, :, 1:, :] - interior[:, :, :-1, :]
    self_block = self_block + gram_sum(change_y * conduct_y, change_y)
    conduct_z = vertical_ratio * harmonic(cell_mobility[:-1], cell_mobility[1:])
    change_z = interior[:, 1:] - interior[:, :-1]
    self_block = self_block + gram_sum(change_z * conduct_z, change_z)
    edges = (
        (
            interior[:, :, :, :1],
            padded_basis[:, :, 1:-1, :1],
            cell_mobility[:, :, :1],
            padded_mobility[:, 1:-1, :1],
        ),
        (
            interior[:, :, :, -1:],
            padded_basis[:, :, 1:-1, -1:],
            cell_mobility[:, :, -1:],
            padded_mobility[:, 1:-1, -1:],
        ),
        (
            interior[:, :, :1, :],
            padded_basis[:, :, :1, 1:-1],
            cell_mobility[:, :1, :],
            padded_mobility[:, :1, 1:-1],
        ),
        (
            interior[:, :, -1:, :],
            padded_basis[:, :, -1:, 1:-1],
            cell_mobility[:, -1:, :],
            padded_mobility[:, -1:, 1:-1],
        ),
    )
    side_blocks = []
    for edge_cells, ghost_cells, edge_mobility, ghost_mobility in edges:
        weighted = edge_cells * harmonic(edge_mobility, ghost_mobility)
        self_block = self_block + gram_sum(weighted, edge_cells)
        side_blocks.append(-gram_sum(weighted, ghost_cells))
    return jnp.stack([self_block] + side_blocks)


def coarse_apply(blocks, vector):
    padded = jnp.pad(vector, ((1, 1), (1, 1), (0, 0)))
    beside = jnp.stack(
        [vector, padded[:-2, 1:-1], padded[2:, 1:-1], padded[1:-1, :-2], padded[1:-1, 2:]], axis=2
    )
    return jnp.einsum("abnkl,abnl->abk", blocks, beside, precision=lax.Precision.HIGHEST)


def coarse_solve(blocks, coarse_source):
    solution = jnp.zeros_like(coarse_source)
    remainder = coarse_source
    direction = coarse_source
    energy = jnp.sum(remainder * remainder)
    for iteration in range(ITERS):
        operator_image = coarse_apply(blocks, direction)
        step_length = energy / (jnp.sum(direction * operator_image) + epsilon)
        solution = solution + step_length * direction
        if iteration + 1 < ITERS:
            remainder = remainder - step_length * operator_image
            renewed = jnp.sum(remainder * remainder)
            direction = remainder + renewed / (energy + epsilon) * direction
            energy = renewed
    return solution


def per_device(basis, mobility, accumulation, residual):
    stacked = jnp.concatenate([basis, mobility[None]], axis=0)
    padded = with_halo(stacked, (("gx", 3), ("gy", 2)), 1)
    padded_basis = padded[:-1].astype(jnp.float32)
    padded_mobility = padded[-1].astype(jnp.float32)
    blocks = face_blocks(padded_basis, padded_mobility, accumulation)
    interior = padded_basis[:, :, 1:-1, 1:-1]
    coarse_source = jnp.einsum("kzyx,zyx->k", interior, residual, precision=lax.Precision.HIGHEST)
    every_block, every_source = (
        lax.all_gather(blocks[None], ("gx", "gy"), axis=0, tiled=True),
        lax.all_gather(coarse_source[None], ("gx", "gy"), axis=0, tiled=True),
    )
    count_x = lax.axis_size("gx")
    count_y = lax.axis_size("gy")
    solution_grid = coarse_solve(
        every_block.reshape(count_x, count_y, 5, K, K), every_source.reshape(count_x, count_y, K)
    )
    anchor = jnp.zeros((), jnp.int32)
    solution = lax.dynamic_slice(
        solution_grid, (lax.axis_index("gx"), lax.axis_index("gy"), anchor), (1, 1, K)
    )[0, 0]
    correction = jnp.einsum("kzyx,k->zyx", interior, solution, precision=lax.Precision.HIGHEST)
    return (correction, solution.reshape(1, 1, K))


def solution(mesh):
    placed = (
        P(None, None, "gy", "gx"),
        P(None, "gy", "gx"),
        P(None, "gy", "gx"),
        P(None, "gy", "gx"),
    )
    return jax.shard_map(
        per_device,
        mesh=mesh,
        in_specs=placed,
        out_specs=(P(None, "gy", "gx"), P("gx", "gy", None)),
        check_vma=False,
    )
```

profile of v0, /device:TPU:1, one launch (start us, length us, event | category | flops | bytes accessed | tf_op | source)
XLA Modules:
  0.0 366.1 jit_solution(8043482095096714497)
XLA Ops:
  7.2 0.0 all-gather.4.cloned.1.call-start
  7.2 1.5 slice_maximum_fusion
  8.8 0.5 copy.292
  9.2 4.5 %collective-permute-start = (bf16[17,4,32,1]{2,1,3,0:T(4,128)(2,1)S(1)}, bf16[17,4,32,1]{2,1,3,0:T(4,128)(2,1)S(1)}, u32[]{:S(2)}, u32[]{:S(2)}) collective-permute-start(bf16[17,4,32,1]{2,1,3,0:T(4,128)(2,1)S(1)} %copy.292), channel_id=1, source_target_pairs={{0,16},{16,32},{32,48},{48,64},{64,80},{80,96},{96,112},{112,128},... | collective-permute-start | bytes 13064 | tf_op jit(solution)/shard_map/ppermute | solution.py:21
  13.7 0.5 copy.293
  14.2 5.5 %collective-permute-start.1 = (bf16[17,4,32,1]{2,1,3,0:T(4,128)(2,1)S(1)}, bf16[17,4,32,1]{2,1,3,0:T(4,128)(2,1)S(1)}, u32[]{:S(2)}, u32[]{:S(2)}) collective-permute-start(bf16[17,4,32,1]{2,1,3,0:T(4,128)(2,1)S(1)} %copy.293), channel_id=1, source_target_pairs={{16,0},{32,16},{48,32},{64,48},{80,64},{96,80},{112,96},{128,112},... | collective-permute-start | bytes 13064 | tf_op jit(solution)/shard_map/ppermute | solution.py:22
  19.8 0.5 copy.239
  20.3 0.3 collective-permute-done.1
  20.6 0.5 copy.240
  21.1 0.4 pad_maximum_fusion.5
  21.6 2.2 collective-permute-start.2
  23.8 1.3 collective-permute-start.3
  25.1 0.3 fusion.73
  25.4 1.2 copy.270
  26.6 1.0 copy.299
  27.6 1.1 copy.298
  28.7 0.1 copy.243
  28.8 0.1 copy.244
  28.9 0.1 maximum_convert_fusion
  29.0 2.5 pad_maximum_fusion
  31.4 0.1 copy.359
  31.5 0.8 fusion.74
  32.2 0.8 add_divide_fusion.1
  33.0 0.8 fusion.75
  33.8 0.2 copy.288
  34.0 0.1 fusion.67
  34.1 1.6 slice_convert_fusion
  35.8 1.9 broadcast_multiply_fusion.1
  37.8 1.9 broadcast_multiply_fusion
  39.7 1.6 broadcast_multiply_fusion.2
  41.4 0.1 fusion.65
  41.4 1.8 slice_multiply_fusion.1
  43.3 1.7 copy.265
  44.9 1.7 copy.261
  46.6 0.2 slice_multiply_fusion.4
  46.8 0.8 convolution_bitcast_fusion.6
  47.7 0.9 convolution_bitcast_fusion.7
  48.6 0.3 slice_multiply_fusion.2
  48.9 1.9 convolution_bitcast_fusion.1
  50.9 2.7 convolution_bitcast_fusion.10
  53.6 2.2 convolution_bitcast_fusion
  55.9 0.1 convolution_bitcast_fusion.8
  56.0 0.1 convolution_bitcast_fusion.9
  56.2 2.9 fusion.24
  59.1 0.1 fusion.15
  59.2 0.1 fusion.12
  59.4 0.9 slice.251
  60.2 0.1 fusion.9
  60.4 0.9 slice.252
  61.2 0.1 fusion.6
  61.4 0.6 copy-done.20
  62.0 0.9 convolution_bitcast_fusion.12
  63.0 0.2 dynamic-update-slice
  63.2 112.0 %all-reduce.2 = f32[8192]{0:T(1024)S(1)} all-reduce(f32[8192]{0:T(1024)S(1)} %dynamic-update-slice), channel_id=2, replica_groups=mesh['gx'=32,'gy'=16] {'gx','gy'}, use_global_device_ids=true, to_apply=%add.2 | all-reduce | flops 8192 | bytes 65536
  175.2 0.1 reshape.68
  175.3 0.1 stack_reshape.3
  175.4 0.6 multiply_reduce_fusion.3
  176.9 116.1 %all-gather.4.cloned.1.call-done = f32[2560,16,16]{2,1,0:T(8,128)} async-done(((f32[5,16,16]{2,1,0:T(8,128)}), f32[2560,16,16]{2,1,0:T(8,128)}) %all-gather.4.cloned.1.call-update) | async-done | bytes 2621456 | tf_op jit(solution)/shard_map/all_gather | solution.py:116
  292.9 29.8 %fusion.2 = f32[32,16,1,16,1]{3,2,4,1,0:T(1,128)S(1)} fusion(f32[32,16,5,16,16]{4,3,2,1,0:T(8,128)} %bitcast.214, f32[32,16,5,16,1]{3,1,0,2,4:T(8,128)S(1)} %bitcast.220), kind=kOutput, calls=%fused_computation.4 | convolution fusion | flops 7864320 | bytes 2818048 | tf_op jit(solution)/shard_map/abnkl,abnl->abk/dot_general | solution.py:87
  322.7 0.7 multiply_reduce_fusion.2
  324.7 0.7 multiply_reduce_fusion.1
  326.2 29.8 %fusion = f32[32,16,1,16,1]{3,2,4,1,0:T(1,128)S(1)} fusion(f32[32,16,5,16,16]{4,3,2,1,0:T(8,128)} %bitcast.215, f32[32,16,5,16,1]{3,1,0,2,4:T(8,128)S(1)} %bitcast.219), kind=kOutput, calls=%fused_computation.2 | convolution fusion | flops 7864320 | bytes 2818048 | tf_op jit(solution)/shard_map/abnkl,abnl->abk/dot_general | solution.py:87
  356.0 0.7 multiply_reduce_fusion
  358.1 1.2 fusion.32
  (68 shorter events, 0.6 us)
Async XLA Ops:
  7.2 54.9 %copy-start = (f32[4,32,128]{2,1,0:T(8,128)S(1)}, f32[4,32,128]{2,1,0:T(8,128)}, u32[]{:S(2)}) copy-start(f32[4,32,128]{2,1,0:T(8,128)} %param.7) | copy-start | bytes 196612
  7.2 285.7 %all-gather.4.cloned.1.call-start = ((), (), s32[]{:S(2)}) async-start(), calls=%async_computation | async-start | bytes 21012480 | tf_op jit(solution)/shard_map/all_gather | solution.py:116
  8.7 12.4 %copy-start.1 = (bf16[16,4,32,128]{3,2,1,0:T(8,128)(2,1)S(1)}, bf16[16,4,32,128]{3,2,1,0:T(8,128)(2,1)}, u32[]{:S(2)}) copy-start(bf16[16,4,32,128]{3,2,1,0:T(8,128)(2,1)} %param.4) | copy-start | bytes 1572868
  8.7 12.4 %copy-start.8 = (bf16[4,32,128]{2,1,0:T(8,128)(2,1)S(1)}, bf16[4,32,128]{2,1,0:T(8,128)(2,1)}, u32[]{:S(2)}) copy-start(bf16[4,32,128]{2,1,0:T(8,128)(2,1)} %param.5) | copy-start | bytes 98308
  9.2 10.5 %collective-permute-start = (bf16[17,4,32,1]{2,1,3,0:T(4,128)(2,1)S(1)}, bf16[17,4,32,1]{2,1,3,0:T(4,128)(2,1)S(1)}, u32[]{:S(2)}, u32[]{:S(2)}) collective-permute-start(bf16[17,4,32,1]{2,1,3,0:T(4,128)(2,1)S(1)} %copy.292), channel_id=1, source_target_pairs={{0,16},{16,32},{32,48},{48,64},{64,80},{80,96},{96,112},{112,128},... | collective-permute-start | bytes 13064 | tf_op jit(solution)/shard_map/ppermute | solution.py:21
  14.2 6.4 %collective-permute-start.1 = (bf16[17,4,32,1]{2,1,3,0:T(4,128)(2,1)S(1)}, bf16[17,4,32,1]{2,1,3,0:T(4,128)(2,1)S(1)}, u32[]{:S(2)}, u32[]{:S(2)}) collective-permute-start(bf16[17,4,32,1]{2,1,3,0:T(4,128)(2,1)S(1)} %copy.293), channel_id=1, source_target_pairs={{16,0},{32,16},{48,32},{64,48},{80,64},{96,80},{112,96},{128,112},... | collective-permute-start | bytes 13064 | tf_op jit(solution)/shard_map/ppermute | solution.py:22
  19.8 8.9 %copy-start.15 = (bf16[17,4,32,1]{2,1,3,0:T(4,128)(2,1)}, bf16[17,4,32,1]{2,1,3,0:T(4,128)(2,1)S(1)}, u32[]{:S(2)}) copy-start(bf16[17,4,32,1]{2,1,3,0:T(4,128)(2,1)S(1)} %collective-permute-done) | copy-start | bytes 13060
  20.6 8.1 %copy-start.16 = (bf16[17,4,32,1]{2,1,3,0:T(4,128)(2,1)}, bf16[17,4,32,1]{2,1,3,0:T(4,128)(2,1)S(1)}, u32[]{:S(2)}) copy-start(bf16[17,4,32,1]{2,1,3,0:T(4,128)(2,1)S(1)} %collective-permute-done.1) | copy-start | bytes 13060
  21.6 7.1 %collective-permute-start.2 = (bf16[17,4,1,130]{3,1,2,0:T(4,128)(2,1)S(1)}, bf16[17,4,1,130]{3,1,2,0:T(4,128)(2,1)S(1)}, u32[]{:S(2)}, u32[]{:S(2)}) collective-permute-start(bf16[17,4,1,130]{3,1,2,0:T(4,128)(2,1)S(1)} %copy.241), channel_id=1, source_target_pairs={{0,1},{1,2},{2,3},{3,4},{4,5},{5,6},{6,7},{7,8},{8,9},{9,10},{10,1... | collective-permute-start | bytes 53048 | tf_op jit(solution)/shard_map/ppermute | solution.py:21
  23.8 4.9 %collective-permute-start.3 = (bf16[17,4,1,130]{3,1,2,0:T(4,128)(2,1)S(1)}, bf16[17,4,1,130]{3,1,2,0:T(4,128)(2,1)S(1)}, u32[]{:S(2)}, u32[]{:S(2)}) collective-permute-start(bf16[17,4,1,130]{3,1,2,0:T(4,128)(2,1)S(1)} %copy.242), channel_id=1, source_target_pairs={{1,0},{2,1},{3,2},{4,3},{5,4},{6,5},{7,6},{8,7},{9,8},{10,9},{11,1... | collective-permute-start | bytes 53048 | tf_op jit(solution)/shard_map/ppermute | solution.py:22
  28.7 2.7 copy-start.13
  28.8 2.7 copy-start.14
  34.1 1.7 copy-start.12
  34.1 1.7 copy-start.9
  37.8 1.9 copy-start.10
  37.8 1.9 copy-start.11
  43.2 5.3 %copy-start.17 = (f32[4,32,128]{2,1,0:T(8,128)S(1)}, f32[4,32,128]{2,1,0:T(8,128)}, u32[]{:S(2)}) copy-start(f32[4,32,128]{2,1,0:T(8,128)} %param.6) | copy-start | bytes 196612
  48.6 2.3 copy-start.5
  48.9 1.9 copy-start.4
  50.8 2.8 copy-start.6
  50.8 2.8 copy-start.7
  50.9 5.0 %copy-start.18 = (bf16[16,4,32,1]{2,0,1,3:T(8,128)(2,1)S(1)}, bf16[16,4,32,1]{2,0,1,3:T(8,128)(2,1)}, u32[]{:S(2)}) copy-start(bf16[16,4,32,1]{2,0,1,3:T(8,128)(2,1)} %copy.299) | copy-start | bytes 12292
  50.9 5.1 %copy-start.19 = (bf16[16,4,32,1]{2,0,1,3:T(8,128)(2,1)S(1)}, bf16[16,4,32,1]{2,0,1,3:T(8,128)(2,1)}, u32[]{:S(2)}) copy-start(bf16[16,4,32,1]{2,0,1,3:T(8,128)(2,1)} %copy.298) | copy-start | bytes 12292
  50.9 5.2 %copy-start.3 = (f32[16,4,32,127]{3,2,1,0:T(8,128)S(1)}, f32[16,4,32,127]{3,2,1,0:T(8,128)}, u32[]{:S(2)}) copy-start(f32[16,4,32,127]{3,2,1,0:T(8,128)} %get-tuple-element.5) | copy-start | bytes 3121156
  53.6 2.5 copy-start.2
  55.8 3.3 slice-start
  55.8 3.4 slice-start.1
  61.4 0.6 copy-start.20
  358.0 1.2 copy-start.21
Sparse Core Ops, SparseCore 0:
  62.1 230.7 all-gather.3
where the time goes:
time: 367 us; the launch traced here: 366 us
  waiting for transfers between devices  116 us (32%)
  blocking collectives  112 us (31%)
  matrix products  73.9 us (20%)
  between operations  18.5 us (5%)
  other arithmetic  17.7 us (5%)
  local copies, waits for them, and re-layouts  14.1 us (4%)
  starting transfers between devices  13.6 us (4%)
    all_gather x1, waiting for transfers between devices, per_device(): lax.all_gather(blocks[None], ('gx', 'gy'), axis=0, tiled=True)  116 us
    unnamed x1, blocking collectives  112 us
    dot_general x2, matrix products, coarse_apply(): jnp.einsum('abnkl,abnl->abk', blocks, beside, precision=lax.Precision.HIG...  59.6 us
    dot_general x12, matrix products, gram_sum(): jnp.einsum('kzyx,lzyx->kl', weighted, other, precision=lax.Precision.HIGH...  12.2 us
  transfers between devices with their start and end apart: 5, of which 2 were waited for; matrix products, arithmetic and copies ran while one was open for 2% of the time, Pallas kernels for 0%

commit v1 on v0

v1 whole, which is shorter than its diff:
```python
import functools

import jax
import jax.numpy as jnp
from jax import lax
from jax.experimental import pallas as pl
from jax.experimental.pallas import tpu as pltpu
from jax.sharding import PartitionSpec as P


K = 16
EPS = 1e-06
VERTICAL = 0.1
MESH = pl.DeviceIdType.MESH
F32 = jnp.float32


def harmonic(a, b):
    return 2.0 * a * b / (a + b)


def lane_edges(x, lane, side):
    tiles = x.reshape(-1, 8, 128)
    out = jnp.zeros((8, 128), F32)
    for j in range(tiles.shape[0]):
        out = jnp.where(lane == j, tiles[j][:, side : side + 1], out)
    return out


def total(x):
    return jnp.sum(jnp.sum(x, axis=0, keepdims=True), axis=1, keepdims=True)


def kernel(
    nx, ny, basis_hbm, mob_hbm, acc_hbm, res_hbm, corr_ref, coarse_ref,
    basis, mob, acc, res, load_sem,
    coef, parts, zx, zy, hsend, ghost, hs_sem, hr_sem,
    row_a, slots_a, row_b, slots_b, ga_sem, gb_sem,
):
    gx, gy = lax.axis_index("gx"), lax.axis_index("gy")
    right, left = lax.rem(gx + 1, nx), lax.rem(gx + nx - 1, nx)
    above, below = lax.rem(gy + 1, ny), lax.rem(gy + ny - 1, ny)

    loads = [
        pltpu.make_async_copy(mob_hbm, mob, load_sem.at[0]),
        pltpu.make_async_copy(res_hbm, res, load_sem.at[1]),
        pltpu.make_async_copy(basis_hbm, basis, load_sem.at[2]),
        pltpu.make_async_copy(acc_hbm, acc, load_sem.at[3]),
    ]
    for c in loads:
        c.start()

    barrier = pltpu.get_barrier_semaphore()

    def greet_y(i, _):
        pl.semaphore_signal(barrier, 1, device_id=(gx, lax.rem(gy + i, ny)), device_id_type=MESH)
        return 0

    def greet_x(i, _):
        pl.semaphore_signal(barrier, 1, device_id=(lax.rem(gx + i, nx), gy), device_id_type=MESH)
        return 0

    lax.fori_loop(1, ny, greet_y, 0)
    lax.fori_loop(1, nx, greet_x, 0)

    lane = lax.broadcasted_iota(jnp.int32, (8, 128), 1)
    sub = lax.broadcasted_iota(jnp.int32, (8, 128), 0)
    cz, cy, cx = mob.shape

    loads[0].wait()
    m = mob[...].astype(F32)
    m_east, m_west = lane_edges(m, lane, cx - 1), lane_edges(m, lane, 0)
    for z in range(cz):
        hsend[0, 2, cz + z : cz + z + 1] = m[z, cy - 1 : cy]
        hsend[0, 3, cz + z : cz + z + 1] = m[z, 0:1]
    loads[1].wait()
    loads[2].wait()
    r = res[...]
    for k in range(K):
        parts[k] = jnp.sum((basis[k].astype(F32) * r).reshape(-1, 8, 128), axis=0)
    b = jnp.sum(jnp.sum(parts[...], axis=1), axis=1, keepdims=True)
    coef[0] = jnp.broadcast_to(b, (K, 128))

    def prolong(which):
        p = jnp.zeros((cz, cy, cx), F32)
        for k in range(K):
            p = p + basis[k].astype(F32) * coef[which, k : k + 1].reshape(1, 1, 128)
        return p

    p0 = prolong(0)
    p0_east, p0_west = lane_edges(p0, lane, cx - 1), lane_edges(p0, lane, 0)
    shifted = (lane >= 16) & (lane < 32)
    hsend[0, 0] = jnp.where(shifted, pltpu.roll(m_east, 16, 1), p0_east)
    hsend[0, 1] = jnp.where(shifted, pltpu.roll(m_west, 16, 1), p0_west)
    for z in range(cz):
        hsend[0, 2, z : z + 1] = p0[z, cy - 1 : cy]
        hsend[0, 3, z : z + 1] = p0[z, 0:1]

    pl.semaphore_wait(barrier, nx + ny - 2)

    def halo(step):
        to = [(right, gy), (left, gy), (gx, above), (gx, below)]
        return [
            pltpu.make_async_remote_copy(
                hsend.at[step, s], ghost.at[step, s ^ 1],
                hs_sem.at[step, s], hr_sem.at[step, s ^ 1],
                device_id=to[s], device_id_type=MESH,
            )
            for s in range(4)
        ]

    first = halo(0)
    for c in first:
        c.start()

    tx = harmonic(m, pltpu.roll(m, cx - 1, 2))
    lane3 = lax.broadcasted_iota(jnp.int32, (cz, cy, cx), 2)
    row3 = lax.broadcasted_iota(jnp.int32, (cz, cy, cx), 1)
    tx = jnp.where(lane3 == cx - 1, 0.0, tx)
    ty = jnp.where(row3 == cy - 1, 0.0, harmonic(m, pltpu.roll(m, cy - 1, 1)))
    tz = VERTICAL * harmonic(m[:-1], m[1:])
    loads[3].wait()
    ac = acc[...]

    def differences(p):
        return p - pltpu.roll(p, cx - 1, 2), p - pltpu.roll(p, cy - 1, 1), p[:-1] - p[1:]

    d0x, d0y, d0z = differences(p0)
    fx, fy, fz = tx * d0x, ty * d0y, tz * d0z
    jp = ac * p0 + (fx - pltpu.roll(fx, 1, 2)) + (fy - pltpu.roll(fy, 1, 1))
    none = jnp.zeros((1, cy, cx), F32)
    jp = jp + jnp.concatenate([fz, none], axis=0) - jnp.concatenate([none, fz], axis=0)
    for k in range(K):
        zk = basis[k].astype(F32)
        parts[k] = jnp.sum((zk * jp).reshape(-1, 8, 128), axis=0)
        zx[k, 0] = lane_edges(zk, lane, cx - 1)
        zx[k, 1] = lane_edges(zk, lane, 0)
        zero = jnp.zeros((cz, 128), F32)
        zy[k, 0] = jnp.concatenate([zk[z, cy - 1 : cy] for z in range(cz)] + [zero], axis=0)
        zy[k, 1] = jnp.concatenate([zk[z, 0:1] for z in range(cz)] + [zero], axis=0)

    has = [gx < nx - 1, gx > 0, gy < ny - 1, gy > 0]
    edge_p0 = [p0_east, p0_west, hsend[0, 2], hsend[0, 3]]

    for c in first:
        c.wait_recv()
    t_edge, flux = [], []
    for s in range(4):
        g = ghost[0, s]
        if s < 2:
            mine, other = (m_east, m_west)[s], pltpu.roll(g, 128 - 16, 1)
            inside = lane < 16
        else:
            mine, other = pltpu.roll(edge_p0[s], 8 - cz, 0), pltpu.roll(g, 8 - cz, 0)
            inside = sub < cz
        t = jnp.where(inside & has[s], harmonic(mine, other), 0.0)
        t_edge.append(t)
        flux.append(t * (edge_p0[s] - g))
    for k in range(K):
        parts[k] = parts[k] + (zx[k, 0] * flux[0] + zx[k, 1] * flux[1]) + (
            zy[k, 0] * flux[2] + zy[k, 1] * flux[3]
        )
    q = jnp.sum(jnp.sum(parts[...], axis=1), axis=1, keepdims=True)
    coef[1] = jnp.broadcast_to(q, (K, 128))

    edge_p1 = [jnp.zeros((8, 128), F32) for _ in range(4)]
    for k in range(K):
        qk = coef[1, k : k + 1]
        edge_p1[0] = edge_p1[0] + zx[k, 0] * qk
        edge_p1[1] = edge_p1[1] + zx[k, 1] * qk
        edge_p1[2] = edge_p1[2] + zy[k, 0] * qk
        edge_p1[3] = edge_p1[3] + zy[k, 1] * qk
    for s in range(4):
        hsend[1, s] = edge_p1[s]
    second = halo(1)
    for c in second:
        c.start()

    bv, qv = coef[0], coef[1]
    qq = jnp.sum(qv * qv, axis=0, keepdims=True)
    bq = jnp.sum(bv * qv, axis=0, keepdims=True)
    bb = jnp.sum(bv * bv, axis=0, keepdims=True)
    ratio = jnp.where(qq > 0.0, bq / jnp.where(qq > 0.0, qq, 1.0), 0.0)
    rest = bv - ratio * qv
    rr = jnp.sum(rest * rest, axis=0, keepdims=True)

    p1 = prolong(1)
    d1x, d1y, d1z = differences(p1)
    ratio3 = ratio.reshape(1, 1, 128)
    pr = p0 - ratio3 * p1
    rx, ry, rz = d0x - ratio3 * d1x, d0y - ratio3 * d1y, d0z - ratio3 * d1z

    def inside_energy(a, ax, ay, az, c, cxx, cyy, czz):
        e = ac * a * c + tx * ax * cxx + ty * ay * cyy
        return jnp.sum(e.reshape(-1, 8, 128), axis=0) + jnp.sum(
            (tz * az * czz).reshape(-1, 8, 128), axis=0
        )

    e_rr = inside_energy(pr, rx, ry, rz, pr, rx, ry, rz)
    e_rp = inside_energy(pr, rx, ry, rz, p1, d1x, d1y, d1z)
    e_pp = inside_energy(p1, d1x, d1y, d1z, p1, d1x, d1y, d1z)

    for c in second:
        c.wait_recv()
    for s in range(4):
        dp = edge_p1[s] - ghost[1, s]
        dr = (edge_p0[s] - ghost[0, s]) - ratio * dp
        half = 0.5 * t_edge[s]
        e_rr = e_rr + half * dr * dr
        e_rp = e_rp + half * dr * dp
        e_pp = e_pp + half * dp * dp

    lane1 = lax.broadcasted_iota(jnp.int32, (1, 128), 1)
    row = jnp.zeros((1, 128), F32)
    for i, v in enumerate([bb, bq, rr, ratio, qq, total(e_rr), total(e_rp), total(e_pp)]):
        row = jnp.where(lane1 == gy * 8 + i, v, row)
    row_a[...] = row

    def send_y(i, _):
        h = (i + 1) // 2
        far = ny // 2 + lax.rem(i, 2) * 2 * h - h
        pltpu.make_async_remote_copy(
            row_a, slots_a.at[gy], ga_sem.at[0], ga_sem.at[1],
            device_id=(gx, lax.rem(gy + far, ny)), device_id_type=MESH,
        ).start()
        return 0

    lax.fori_loop(0, ny - 1, send_y, 0)
    some = slots_a.at[pl.ds(0, ny - 1)]
    pltpu.make_async_copy(some, some, ga_sem.at[1]).wait()
    for i in range(ny):
        row = row + jnp.where(gy == i, 0.0, slots_a[i])
    row_b[...] = row

    def send_x(i, _):
        pltpu.make_async_remote_copy(
            row_b, slots_b.at[gx], gb_sem.at[0], gb_sem.at[1],
            device_id=(lax.rem(gx + i, nx), gy), device_id_type=MESH,
        ).start()
        return 0

    lax.fori_loop(1, nx, send_x, 0)
    some_b = slots_b.at[pl.ds(0, nx - 1)]
    pltpu.make_async_copy(some_b, some_b, gb_sem.at[1]).wait()
    every = jnp.concatenate(
        [jnp.where(gx == i, row, slots_b[i]) for i in range(nx)], axis=0
    )
    lanes = lax.rem(lax.broadcasted_iota(jnp.int32, (nx, 128), 1), 8)

    def over_all(x, i):
        return total(jnp.where(lanes == i, x, 0.0))

    energy = over_all(every, 0)
    step0 = energy / (over_all(every, 1) + EPS)
    next1, next2 = pltpu.roll(every, 127, 1), pltpu.roll(every, 126, 1)
    off = next1 - step0
    renewed = over_all(every + off * off * next2, 2)
    alpha = 1.0 + renewed / (energy + EPS)
    lean = alpha * pltpu.roll(every, 2, 1) - step0
    curved = alpha * alpha * every + lean * (2.0 * alpha * next1 + lean * next2)
    step1 = renewed / (over_all(curved, 5) + EPS)
    c0, c1 = step0 + step1 * alpha, -(step1 * step0)

    corr_ref[...] = c0.reshape(1, 1, 1) * p0 + c1.reshape(1, 1, 1) * p1
    x = c0 * coef[0] + c1 * coef[1]
    diag = lax.broadcasted_iota(jnp.int32, (K, 128), 0) == lax.broadcasted_iota(jnp.int32, (K, 128), 1)
    coarse_ref[0] = jnp.sum(jnp.where(diag, x, 0.0), axis=0, keepdims=True)[:, :K]

    for c in first + second:
        c.wait_send()
    pltpu.make_async_copy(some, some, ga_sem.at[0]).wait()
    pltpu.make_async_copy(some_b, some_b, gb_sem.at[0]).wait()


def solution(mesh):
    nx, ny = mesh.shape["gx"], mesh.shape["gy"]

    def per_device(basis, mobility, accumulation, residual):
        cells = mobility.shape
        vmem = pltpu.VMEM
        return pl.pallas_call(
            functools.partial(kernel, nx, ny),
            out_shape=(
                jax.ShapeDtypeStruct(cells, F32),
                jax.ShapeDtypeStruct((1, 1, K), F32),
            ),
            in_specs=[pl.BlockSpec(memory_space=pl.ANY)] * 4,
            out_specs=(pl.BlockSpec(memory_space=pltpu.VMEM),) * 2,
            scratch_shapes=[
                vmem(basis.shape, basis.dtype),
                vmem(cells, mobility.dtype),
                vmem(cells, F32),
                vmem(cells, F32),
                pltpu.SemaphoreType.DMA((4,)),
                vmem((2, K, 128), F32),
                vmem((K, 8, 128), F32),
                vmem((K, 2, 8, 128), F32),
                vmem((K, 2, 8, 128), F32),
                vmem((2, 4, 8, 128), F32),
                vmem((2, 4, 8, 128), F32),
                pltpu.SemaphoreType.DMA((2, 4)),
                pltpu.SemaphoreType.DMA((2, 4)),
                vmem((1, 128), F32),
                vmem((ny, 1, 128), F32),
                vmem((1, 128), F32),
                vmem((nx, 1, 128), F32),
                pltpu.SemaphoreType.DMA((2,)),
                pltpu.SemaphoreType.DMA((2,)),
            ],
            compiler_params=pltpu.CompilerParams(collective_id=0, has_side_effects=True),
        )(basis, mobility, accumulation, residual)

    cells = P(None, "gy", "gx")
    return jax.shard_map(
        per_device,
        mesh=mesh,
        in_specs=(P(None, None, "gy", "gx"), cells, cells, cells),
        out_specs=(cells, P("gx", "gy", None)),
        check_vma=False,
    )
```

time: 367 us -> 39.3 us (0.11)
  waiting for transfers between devices: 116 us -> 0 us
  blocking collectives: 112 us -> 0 us
  matrix products: 73.9 us -> 0 us
  Pallas kernels: 0 us -> 36.5 us
  between operations: 18.5 us -> 0.65 us
  other arithmetic: 17.7 us -> 0 us
  starting transfers between devices: 13.6 us -> 0 us
  local copies, waits for them, and re-layouts: 14.1 us -> 1.99 us
    all_gather x1 -> x0, waiting for transfers between devices: 116 us -> none  [per_device(): lax.all_gather(blocks[None], ('gx', 'gy'), axis=0, tiled=True)]
    unnamed x1 -> x0, blocking collectives: 112 us -> none
    dot_general x16 -> x0, matrix products: 73.9 us -> none  [the longest x2 59.6 us: coarse_apply(): jnp.einsum('abnkl,abnl->abk', blocks, beside, precision=lax.Precision.HIG...]
    pallas_call x0 -> x1, Pallas kernels: none -> 36.5 us  [per_device(): pl.pallas_call(functools.partial(kernel, nx, ny), out_shape=(jax.ShapeDty...]
    ppermute x4 -> x0, starting transfers between devices: 13.6 us -> none  [the longest x2 6.83 us: with_halo(): after = lax.ppermute(initial, axis, down)]
    mul x9 -> x0, other arithmetic: 8.05 us -> none  [the longest x4 2.18 us: face_blocks(): weighted = edge_cells * harmonic(edge_mobility, ghost_mobility)]
    concatenate x2 -> x0, other arithmetic: 3.97 us -> none  [the longest x1 2.46 us: with_halo(): x = jnp.concatenate([before, x, after], axis=dim)]
  transfers between devices with their start and end apart: 5 -> 0, of which waited for: 2 -> 0; matrix products, arithmetic and copies ran while one was open for 2% -> 0% of each run, Pallas kernels for 0% -> 0%
where the time goes in v1:
time: 39.3 us; the launch traced here: 39.1 us
  Pallas kernels  36.5 us (93%)
  local copies, waits for them, and re-layouts  1.99 us (5%)
  between operations  0.65 us (2%)
    pallas_call x1, Pallas kernels, per_device(): pl.pallas_call(functools.partial(kernel, nx, ny), out_shape=(jax.ShapeDty...  36.5 us
    unnamed x4, local copies, waits for them, and re-layouts  1.99 us

profile of v1, /device:TPU:1, one launch (start us, length us, event | category | flops | bytes accessed | tf_op | source)
XLA Modules:
  0.0 39.1 jit_solution(8551647335743254919)
XLA Ops:
  0.6 36.5 %shard_map.59 = (f32[4,32,128]{2,1,0:T(8,128)}, f32[1,1,16]{2,1,0:T(1,128)}) custom-call(bf16[16,4,32,128]{3,2,1,0:T(8,128)(2,1)} %basis_hbm.1, bf16[4,32,128]{2,1,0:T(8,128)(2,1)} %mob_hbm.1, f32[4,32,128]{2,1,0:T(8,128)} %acc_hbm.1, f32[4,32,128]{2,1,0:T(8,128)} %res_hbm.1), custom_call_target="tpu_custom_call" | custom-call | tf_op jit(solution)/shard_map/pallas_call | solution.py:281
  37.1 0.0 copy-start
  37.1 1.5 %copy.8 = f32[4,32,128]{2,1,0:T(8,128)} copy(f32[4,32,128]{2,1,0:T(8,128)} %get-tuple-element.4) | data formatting | bytes 131072
  38.6 0.0 copy-done
  38.6 0.5 %copy.9 = f32[1,1,16]{2,1,0:T(1,128)} copy(f32[1,1,16]{2,1,0:T(1,128)S(1)} %copy-done) | data formatting | bytes 128
Async XLA Ops:
  37.1 1.5 %copy-start = (f32[1,1,16]{2,1,0:T(1,128)S(1)}, f32[1,1,16]{2,1,0:T(1,128)}, u32[]{:S(2)}) copy-start(f32[1,1,16]{2,1,0:T(1,128)} %get-tuple-element.5) | copy-start | bytes 196

commit v2 on v1

--- a/solution.py
+++ b/solution.py
@@ -31,13 +31,20 @@
     return jnp.sum(jnp.sum(x, axis=0, keepdims=True), axis=1, keepdims=True)
 
 
+def signal(sem, x, y):
+    pl.semaphore_signal(sem, 1, device_id=(x, y), device_id_type=MESH)
+
+
 def kernel(
-    nx, ny, basis_hbm, mob_hbm, acc_hbm, res_hbm, corr_ref, coarse_ref,
+    nx, ny, basis_hbm, mob_hbm, acc_hbm, res_hbm, field, small_ref,
     basis, mob, acc, res, load_sem,
     coef, parts, zx, zy, hsend, ghost, hs_sem, hr_sem,
     row_a, slots_a, row_b, slots_b, ga_sem, gb_sem,
+    far_x, far_y, met,
 ):
     gx, gy = lax.axis_index("gx"), lax.axis_index("gy")
+    chip, core = gx // 2, lax.rem(gx, 2)
+    twin = gx + 1 - 2 * core
     right, left = lax.rem(gx + 1, nx), lax.rem(gx + nx - 1, nx)
     above, below = lax.rem(gy + 1, ny), lax.rem(gy + ny - 1, ny)
 
@@ -51,17 +58,29 @@
         c.start()
 
     barrier = pltpu.get_barrier_semaphore()
-
-    def greet_y(i, _):
-        pl.semaphore_signal(barrier, 1, device_id=(gx, lax.rem(gy + i, ny)), device_id_type=MESH)
-        return 0
-
-    def greet_x(i, _):
-        pl.semaphore_signal(barrier, 1, device_id=(lax.rem(gx + i, nx), gy), device_id_type=MESH)
-        return 0
-
-    lax.fori_loop(1, ny, greet_y, 0)
-    lax.fori_loop(1, nx, greet_x, 0)
+    for x, y in ((right, gy), (left, gy), (gx, above), (gx, below)):
+        signal(barrier, x, y)
+
+    reach_y = [d for d in (1, 2, 4, 8, 16, 32) if d < ny // 2]
+    reach_x = [d for d in (1, 2, 4, 8, 16, 32) if d < nx // 2]
+
+    def tell_y(i):
+        if i < len(reach_y):
+            signal(far_y.at[i], gx, lax.rem(gy + reach_y[i], ny))
+            signal(far_y.at[i], gx, lax.rem(gy + ny - reach_y[i], ny))
+
+    def tell_x(i):
+        if i < len(reach_x):
+            signal(far_x.at[i], lax.rem(gx + reach_x[i], nx), gy)
+            signal(far_x.at[i], lax.rem(gx + nx - reach_x[i], nx), gy)
+
+    def hear_y(i):
+        if i < len(reach_y):
+            pl.semaphore_wait(far_y.at[i], 2)
+
+    def hear_x(i):
+        if i < len(reach_x):
+            pl.semaphore_wait(far_x.at[i], 2)
 
     lane = lax.broadcasted_iota(jnp.int32, (8, 128), 1)
     sub = lax.broadcasted_iota(jnp.int32, (8, 128), 0)
@@ -96,7 +115,7 @@
         hsend[0, 2, z : z + 1] = p0[z, cy - 1 : cy]
         hsend[0, 3, z : z + 1] = p0[z, 0:1]
 
-    pl.semaphore_wait(barrier, nx + ny - 2)
+    pl.semaphore_wait(barrier, 4)
 
     def halo(step):
         to = [(right, gy), (left, gy), (gx, above), (gx, below)]
@@ -112,6 +131,8 @@
     first = halo(0)
     for c in first:
         c.start()
+    tell_y(0)
+    tell_x(0)
 
     tx = harmonic(m, pltpu.roll(m, cx - 1, 2))
     lane3 = lax.broadcasted_iota(jnp.int32, (cz, cy, cx), 2)
@@ -139,11 +160,16 @@
         zy[k, 0] = jnp.concatenate([zk[z, cy - 1 : cy] for z in range(cz)] + [zero], axis=0)
         zy[k, 1] = jnp.concatenate([zk[z, 0:1] for z in range(cz)] + [zero], axis=0)
 
+    field[0] = p0
+    hear_y(0)
+    tell_y(1)
     has = [gx < nx - 1, gx > 0, gy < ny - 1, gy > 0]
     edge_p0 = [p0_east, p0_west, hsend[0, 2], hsend[0, 3]]
 
     for c in first:
         c.wait_recv()
+    hear_x(0)
+    tell_x(1)
     t_edge, flux = [], []
     for s in range(4):
         g = ghost[0, s]
@@ -175,6 +201,8 @@
     second = halo(1)
     for c in second:
         c.start()
+    hear_y(1)
+    tell_y(2)
 
     bv, qv = coef[0], coef[1]
     qq = jnp.sum(qv * qv, axis=0, keepdims=True)
@@ -185,6 +213,7 @@
     rr = jnp.sum(rest * rest, axis=0, keepdims=True)
 
     p1 = prolong(1)
+    field[1] = p1
     d1x, d1y, d1z = differences(p1)
     ratio3 = ratio.reshape(1, 1, 128)
     pr = p0 - ratio3 * p1
@@ -200,6 +229,10 @@
     e_rp = inside_energy(pr, rx, ry, rz, p1, d1x, d1y, d1z)
     e_pp = inside_energy(p1, d1x, d1y, d1z, p1, d1x, d1y, d1z)
 
+    hear_y(2)
+    signal(met, twin, gy)
+    hear_x(1)
+    tell_x(2)
     for c in second:
         c.wait_recv()
     for s in range(4):
@@ -215,35 +248,54 @@
     for i, v in enumerate([bb, bq, rr, ratio, qq, total(e_rr), total(e_rp), total(e_pp)]):
         row = jnp.where(lane1 == gy * 8 + i, v, row)
     row_a[...] = row
-
-    def send_y(i, _):
-        h = (i + 1) // 2
-        far = ny // 2 + lax.rem(i, 2) * 2 * h - h
+    pl.semaphore_wait(met, 1)
+
+    def send_a(x, away):
         pltpu.make_async_remote_copy(
-            row_a, slots_a.at[gy], ga_sem.at[0], ga_sem.at[1],
-            device_id=(gx, lax.rem(gy + far, ny)), device_id_type=MESH,
+            row_a, slots_a.at[core * ny + gy], ga_sem.at[0], ga_sem.at[1],
+            device_id=(x, lax.rem(gy + away, ny)), device_id_type=MESH,
         ).start()
-        return 0
-
-    lax.fori_loop(0, ny - 1, send_y, 0)
-    some = slots_a.at[pl.ds(0, ny - 1)]
+
+    for away in sorted(range(1, ny), key=lambda d: -min(d, ny - d)):
+        send_a(gx, away)
+        send_a(twin, away)
+    send_a(twin, 0)
+    hear_x(2)
+    tell_x(3)
+    some = slots_a.at[pl.ds(0, 2 * ny - 1)]
     pltpu.make_async_copy(some, some, ga_sem.at[1]).wait()
-    for i in range(ny):
-        row = row + jnp.where(gy == i, 0.0, slots_a[i])
-    row_b[...] = row
-
-    def send_x(i, _):
+    for c in range(2):
+        both = jnp.zeros((1, 128), F32)
+        for i in range(ny):
+            both = both + jnp.where((core == c) & (gy == i), row, slots_a[c * ny + i])
+        row_b[c] = both
+
+    hear_x(3)
+    chips = nx // 2
+    ring_x = 4 if chips % 4 == 0 else chips
+    ring_y = chips // ring_x
+    cx0, cy0 = lax.rem(chip, ring_x), chip // ring_x
+
+    def hops(d):
+        return min(d[0], ring_x - d[0]) + min(d[1], ring_y - d[1])
+
+    for dx, dy in sorted(
+        ((i, j) for i in range(ring_x) for j in range(ring_y) if i + j), key=lambda d: -hops(d)
+    ):
+        to = lax.rem(cy0 + dy, ring_y) * ring_x + lax.rem(cx0 + dx, ring_x)
         pltpu.make_async_remote_copy(
-            row_b, slots_b.at[gx], gb_sem.at[0], gb_sem.at[1],
-            device_id=(lax.rem(gx + i, nx), gy), device_id_type=MESH,
+            row_b, slots_b.at[chip], gb_sem.at[0], gb_sem.at[1],
+            device_id=(to * 2 + core, gy), device_id_type=MESH,
         ).start()
-        return 0
-
-    lax.fori_loop(1, nx, send_x, 0)
-    some_b = slots_b.at[pl.ds(0, nx - 1)]
+    some_b = slots_b.at[pl.ds(0, chips - 1)]
     pltpu.make_async_copy(some_b, some_b, gb_sem.at[1]).wait()
     every = jnp.concatenate(
-        [jnp.where(gx == i, row, slots_b[i]) for i in range(nx)], axis=0
+        [
+            jnp.where(chip == i, row_b[c], slots_b[i, c])
+            for i in range(chips)
+            for c in range(2)
+        ],
+        axis=0,
     )
     lanes = lax.rem(lax.broadcasted_iota(jnp.int32, (nx, 128), 1), 8)
 
@@ -261,10 +313,11 @@
     step1 = renewed / (over_all(curved, 5) + EPS)
     c0, c1 = step0 + step1 * alpha, -(step1 * step0)
 
-    corr_ref[...] = c0.reshape(1, 1, 1) * p0 + c1.reshape(1, 1, 1) * p1
     x = c0 * coef[0] + c1 * coef[1]
     diag = lax.broadcasted_iota(jnp.int32, (K, 128), 0) == lax.broadcasted_iota(jnp.int32, (K, 128), 1)
-    coarse_ref[0] = jnp.sum(jnp.where(diag, x, 0.0), axis=0, keepdims=True)[:, :K]
+    small_ref[0:1] = jnp.sum(jnp.where(diag, x, 0.0), axis=0, keepdims=True)
+    small_ref[1:2] = jnp.broadcast_to(c0, (1, 128))
+    small_ref[2:3] = jnp.broadcast_to(c1, (1, 128))
 
     for c in first + second:
         c.wait_send()
@@ -278,11 +331,11 @@
     def per_device(basis, mobility, accumulation, residual):
         cells = mobility.shape
         vmem = pltpu.VMEM
-        return pl.pallas_call(
+        field, small = pl.pallas_call(
             functools.partial(kernel, nx, ny),
             out_shape=(
-                jax.ShapeDtypeStruct(cells, F32),
-                jax.ShapeDtypeStruct((1, 1, K), F32),
+                vmem((2, *cells), F32),
+                vmem((8, 128), F32),
             ),
             in_specs=[pl.BlockSpec(memory_space=pl.ANY)] * 4,
             out_specs=(pl.BlockSpec(memory_space=pltpu.VMEM),) * 2,
@@ -301,14 +354,27 @@
                 pltpu.SemaphoreType.DMA((2, 4)),
                 pltpu.SemaphoreType.DMA((2, 4)),
                 vmem((1, 128), F32),
-                vmem((ny, 1, 128), F32),
-                vmem((1, 128), F32),
-                vmem((nx, 1, 128), F32),
+                vmem((2 * ny, 1, 128), F32),
+                vmem((2, 1, 128), F32),
+                vmem((nx // 2, 2, 1, 128), F32),
                 pltpu.SemaphoreType.DMA((2,)),
                 pltpu.SemaphoreType.DMA((2,)),
+                pltpu.SemaphoreType.REGULAR((4,)),
+                pltpu.SemaphoreType.REGULAR((4,)),
+                pltpu.SemaphoreType.REGULAR,
             ],
             compiler_params=pltpu.CompilerParams(collective_id=0, has_side_effects=True),
         )(basis, mobility, accumulation, residual)
+
+        def finish(f, s, corr, coarse):
+            corr[...] = s[1:2].reshape(1, 1, 128) * f[0] + s[2:3].reshape(1, 1, 128) * f[1]
+            coarse[0] = s[0:1, :K]
+
+        return pl.pallas_call(
+            finish,
+            out_shape=(jax.ShapeDtypeStruct(cells, F32), jax.ShapeDtypeStruct((1, 1, K), F32)),
+            in_specs=[pl.BlockSpec(memory_space=pltpu.VMEM)] * 2,
+        )(*(pltpu.with_memory_space_constraint(v, pltpu.VMEM) for v in (field, small)))
 
     cells = P(None, "gy", "gx")
     return jax.shard_map(

time: 39.3 us -> 33.8 us (0.86)
  Pallas kernels: 36.5 us -> 33 us
  local copies, waits for them, and re-layouts: 1.99 us -> 0 us
    pallas_call x1 -> x2, Pallas kernels: 36.5 us -> 33 us  [the longest x1 32.3 us: per_device(): pl.pallas_call(functools.partial(kernel, nx, ny), out_shape=(vmem((2, *ce...]
    unnamed x4 -> x0, local copies, waits for them, and re-layouts: 1.99 us -> none
where the time goes in v2:
time: 33.8 us; the launch traced here: 33.6 us
  Pallas kernels  33 us (98%)
  between operations  0.64 us (2%)
    pallas_call x1, Pallas kernels, per_device(): pl.pallas_call(functools.partial(kernel, nx, ny), out_shape=(vmem((2, *ce...  32.3 us

profile of v2, /device:TPU:1, one launch (start us, length us, event | category | flops | bytes accessed | tf_op | source)
XLA Modules:
  0.0 33.6 jit_solution(4999418876898927214)
XLA Ops:
  0.6 32.3 %shard_map.59 = (f32[2,4,32,128]{3,2,1,0:T(8,128)S(1)}, f32[8,128]{1,0:T(8,128)S(1)}) custom-call(bf16[16,4,32,128]{3,2,1,0:T(8,128)(2,1)} %basis_hbm.1, bf16[4,32,128]{2,1,0:T(8,128)(2,1)} %mob_hbm.1, f32[4,32,128]{2,1,0:T(8,128)} %acc_hbm.1, f32[4,32,128]{2,1,0:T(8,128)} %res_hbm.1), custom_call_target="tpu_custom_call" | custom-call | tf_op jit(solution)/shard_map/pallas_call | solution.py:334
  33.0 0.6 %shard_map.60 = (f32[4,32,128]{2,1,0:T(8,128)}, f32[1,1,16]{2,1,0:T(1,128)}) custom-call(f32[2,4,32,128]{3,2,1,0:T(8,128)S(1)} %get-tuple-element.4.f, f32[8,128]{1,0:T(8,128)S(1)} %get-tuple-element.5.s), custom_call_target="tpu_custom_call" | custom-call | tf_op jit(solution)/shard_map/pallas_call | solution.py:373

commit v3 on v2

--- a/solution.py
+++ b/solution.py
@@ -45,24 +45,43 @@
     gx, gy = lax.axis_index("gx"), lax.axis_index("gy")
     chip, core = gx // 2, lax.rem(gx, 2)
     twin = gx + 1 - 2 * core
-    right, left = lax.rem(gx + 1, nx), lax.rem(gx + nx - 1, nx)
-    above, below = lax.rem(gy + 1, ny), lax.rem(gy + ny - 1, ny)
-
+    right, left = gx + 1, gx - 1
+    above, below = gy + 1, gy - 1
+
+    quarters = [pl.ds(k, K // 4) for k in range(0, K, K // 4)]
     loads = [
         pltpu.make_async_copy(mob_hbm, mob, load_sem.at[0]),
         pltpu.make_async_copy(res_hbm, res, load_sem.at[1]),
-        pltpu.make_async_copy(basis_hbm, basis, load_sem.at[2]),
-        pltpu.make_async_copy(acc_hbm, acc, load_sem.at[3]),
+        *(
+            pltpu.make_async_copy(basis_hbm.at[part], basis.at[part], load_sem.at[2 + i])
+            for i, part in enumerate(quarters)
+        ),
+        pltpu.make_async_copy(acc_hbm, acc, load_sem.at[6]),
     ]
     for c in loads:
         c.start()
 
+    has = [gx < nx - 1, gx > 0, gy < ny - 1, gy > 0]
     barrier = pltpu.get_barrier_semaphore()
-    for x, y in ((right, gy), (left, gy), (gx, above), (gx, below)):
-        signal(barrier, x, y)
-
-    reach_y = [d for d in (1, 2, 4, 8, 16, 32) if d < ny // 2]
-    reach_x = [d for d in (1, 2, 4, 8, 16, 32) if d < nx // 2]
+    near_y = [d for d in (1, -1, 2, -2) if 2 * abs(d) < ny]
+    for d in near_y:
+        signal(barrier, gx, lax.rem(gy + ny + d, ny))
+    reach_y = [d for d in (2, 4, 8, 16, 32) if d < ny // 2]
+    reach_x = [d for d in (1, 2, 4, 8, 16, 32) if d < nx]
+
+    def signal_x(sem, d):
+        @pl.when(gx + d < nx)
+        def _():
+            signal(sem, gx + d, gy)
+
+        @pl.when(gx >= d)
+        def _():
+            signal(sem, gx - d, gy)
+
+    def count_x(d):
+        return jnp.where(gx + d < nx, 1, 0) + jnp.where(gx >= d, 1, 0)
+
+    signal_x(barrier, 1)
 
     def tell_y(i):
         if i < len(reach_y):
@@ -71,8 +90,7 @@
 
     def tell_x(i):
         if i < len(reach_x):
-            signal(far_x.at[i], lax.rem(gx + reach_x[i], nx), gy)
-            signal(far_x.at[i], lax.rem(gx + nx - reach_x[i], nx), gy)
+            signal_x(far_x.at[i], reach_x[i])
 
     def hear_y(i):
         if i < len(reach_y):
@@ -80,7 +98,7 @@
 
     def hear_x(i):
         if i < len(reach_x):
-            pl.semaphore_wait(far_x.at[i], 2)
+            pl.semaphore_wait(far_x.at[i], count_x(reach_x[i]))
 
     lane = lax.broadcasted_iota(jnp.int32, (8, 128), 1)
     sub = lax.broadcasted_iota(jnp.int32, (8, 128), 0)
@@ -93,9 +111,10 @@
         hsend[0, 2, cz + z : cz + z + 1] = m[z, cy - 1 : cy]
         hsend[0, 3, cz + z : cz + z + 1] = m[z, 0:1]
     loads[1].wait()
-    loads[2].wait()
     r = res[...]
     for k in range(K):
+        if k % (K // 4) == 0:
+            loads[2 + k // (K // 4)].wait()
         parts[k] = jnp.sum((basis[k].astype(F32) * r).reshape(-1, 8, 128), axis=0)
     b = jnp.sum(jnp.sum(parts[...], axis=1), axis=1, keepdims=True)
     coef[0] = jnp.broadcast_to(b, (K, 128))
@@ -115,7 +134,7 @@
         hsend[0, 2, z : z + 1] = p0[z, cy - 1 : cy]
         hsend[0, 3, z : z + 1] = p0[z, 0:1]
 
-    pl.semaphore_wait(barrier, 4)
+    pl.semaphore_wait(barrier, count_x(1) + len(near_y))
 
     def halo(step):
         to = [(right, gy), (left, gy), (gx, above), (gx, below)]
@@ -128,9 +147,27 @@
             for s in range(4)
         ]
 
+    middle = ny // 2
+    weighs = [has[0], gx < 0, has[2] & (gy < middle), has[3] & (gy > middle)]
+    gives = [gx < 0, has[1], has[2] & (gy >= middle), has[3] & (gy <= middle)]
+
+    def arrive(step, sides):
+        for s in range(4):
+
+            @pl.when(sides[s])
+            def _(s=s):
+                here = ghost.at[step, s]
+                pltpu.make_async_copy(here, here, hr_sem.at[step, s]).wait()
+
+    def each(copies, sides, act):
+        for s in range(4):
+
+            @pl.when(sides[s])
+            def _(c=copies[s]):
+                act(c)
+
     first = halo(0)
-    for c in first:
-        c.start()
+    each(first, has, lambda c: c.start())
     tell_y(0)
     tell_x(0)
 
@@ -140,7 +177,7 @@
     tx = jnp.where(lane3 == cx - 1, 0.0, tx)
     ty = jnp.where(row3 == cy - 1, 0.0, harmonic(m, pltpu.roll(m, cy - 1, 1)))
     tz = VERTICAL * harmonic(m[:-1], m[1:])
-    loads[3].wait()
+    loads[6].wait()
     ac = acc[...]
 
     def differences(p):
@@ -163,14 +200,12 @@
     field[0] = p0
     hear_y(0)
     tell_y(1)
-    has = [gx < nx - 1, gx > 0, gy < ny - 1, gy > 0]
-    edge_p0 = [p0_east, p0_west, hsend[0, 2], hsend[0, 3]]
-
-    for c in first:
-        c.wait_recv()
     hear_x(0)
     tell_x(1)
-    t_edge, flux = [], []
+    edge_p0 = [p0_east, p0_west, hsend[0, 2], hsend[0, 3]]
+
+    arrive(0, has)
+    t_edge, jump, flux = [], [], []
     for s in range(4):
         g = ghost[0, s]
         if s < 2:
@@ -179,9 +214,12 @@
         else:
             mine, other = pltpu.roll(edge_p0[s], 8 - cz, 0), pltpu.roll(g, 8 - cz, 0)
             inside = sub < cz
-        t = jnp.where(inside & has[s], harmonic(mine, other), 0.0)
-        t_edge.append(t)
-        flux.append(t * (edge_p0[s] - g))
+        joined = inside & has[s]
+        t = jnp.where(joined, harmonic(mine, other), 0.0)
+        d = jnp.where(joined, edge_p0[s] - g, 0.0)
+        t_edge.append((joined, t))
+        jump.append(d)
+        flux.append(t * d)
     for k in range(K):
         parts[k] = parts[k] + (zx[k, 0] * flux[0] + zx[k, 1] * flux[1]) + (
             zy[k, 0] * flux[2] + zy[k, 1] * flux[3]
@@ -199,10 +237,7 @@
     for s in range(4):
         hsend[1, s] = edge_p1[s]
     second = halo(1)
-    for c in second:
-        c.start()
-    hear_y(1)
-    tell_y(2)
+    each(second, gives, lambda c: c.start())
 
     bv, qv = coef[0], coef[1]
     qq = jnp.sum(qv * qv, axis=0, keepdims=True)
@@ -229,19 +264,20 @@
     e_rp = inside_energy(pr, rx, ry, rz, p1, d1x, d1y, d1z)
     e_pp = inside_energy(p1, d1x, d1y, d1z, p1, d1x, d1y, d1z)
 
-    hear_y(2)
+    hear_y(1)
     signal(met, twin, gy)
     hear_x(1)
     tell_x(2)
-    for c in second:
-        c.wait_recv()
-    for s in range(4):
-        dp = edge_p1[s] - ghost[1, s]
-        dr = (edge_p0[s] - ghost[0, s]) - ratio * dp
-        half = 0.5 * t_edge[s]
-        e_rr = e_rr + half * dr * dr
-        e_rp = e_rp + half * dr * dp
-        e_pp = e_pp + half * dp * dp
+    arrive(1, weighs)
+    for s in (0, 2, 3):
+        joined, t = t_edge[s]
+        mine = joined & weighs[s]
+        dp = jnp.where(mine, edge_p1[s] - ghost[1, s], 0.0)
+        dr = jump[s] - ratio * dp
+        t = jnp.where(mine, t, 0.0)
+        e_rr = e_rr + t * dr * dr
+        e_rp = e_rp + t * dr * dp
+        e_pp = e_pp + t * dp * dp
 
     lane1 = lax.broadcasted_iota(jnp.int32, (1, 128), 1)
     row = jnp.zeros((1, 128), F32)
@@ -262,7 +298,11 @@
     send_a(twin, 0)
     hear_x(2)
     tell_x(3)
+    hear_x(3)
+    tell_x(4)
     some = slots_a.at[pl.ds(0, 2 * ny - 1)]
+    each(first, has, lambda c: c.wait_send())
+    each(second, gives, lambda c: c.wait_send())
     pltpu.make_async_copy(some, some, ga_sem.at[1]).wait()
     for c in range(2):
         both = jnp.zeros((1, 128), F32)
@@ -270,7 +310,7 @@
             both = both + jnp.where((core == c) & (gy == i), row, slots_a[c * ny + i])
         row_b[c] = both
 
-    hear_x(3)
+    hear_x(4)
     chips = nx // 2
     ring_x = 4 if chips % 4 == 0 else chips
     ring_y = chips // ring_x
@@ -288,6 +328,7 @@
             device_id=(to * 2 + core, gy), device_id_type=MESH,
         ).start()
     some_b = slots_b.at[pl.ds(0, chips - 1)]
+    pltpu.make_async_copy(some, some, ga_sem.at[0]).wait()
     pltpu.make_async_copy(some_b, some_b, gb_sem.at[1]).wait()
     every = jnp.concatenate(
         [
@@ -319,9 +360,6 @@
     small_ref[1:2] = jnp.broadcast_to(c0, (1, 128))
     small_ref[2:3] = jnp.broadcast_to(c1, (1, 128))
 
-    for c in first + second:
-        c.wait_send()
-    pltpu.make_async_copy(some, some, ga_sem.at[0]).wait()
     pltpu.make_async_copy(some_b, some_b, gb_sem.at[0]).wait()
 
 
@@ -344,7 +382,7 @@
                 vmem(cells, mobility.dtype),
                 vmem(cells, F32),
                 vmem(cells, F32),
-                pltpu.SemaphoreType.DMA((4,)),
+                pltpu.SemaphoreType.DMA((7,)),
                 vmem((2, K, 128), F32),
                 vmem((K, 8, 128), F32),
                 vmem((K, 2, 8, 128), F32),
@@ -359,8 +397,8 @@
                 vmem((nx // 2, 2, 1, 128), F32),
                 pltpu.SemaphoreType.DMA((2,)),
                 pltpu.SemaphoreType.DMA((2,)),
-                pltpu.SemaphoreType.REGULAR((4,)),
-                pltpu.SemaphoreType.REGULAR((4,)),
+                pltpu.SemaphoreType.REGULAR((5,)),
+                pltpu.SemaphoreType.REGULAR((2,)),
                 pltpu.SemaphoreType.REGULAR,
             ],
             compiler_params=pltpu.CompilerParams(collective_id=0, has_side_effects=True),

time: 33.8 us -> 33.1 us (0.979)
  Pallas kernels: 33 us -> 32.3 us
    pallas_call x1, Pallas kernels: 32.3 us -> 31.7 us  [per_device(): pl.pallas_call(functools.partial(kernel, nx, ny), out_shape=(vmem((2, *ce...]
where the time goes in v3:
time: 33.1 us; the launch traced here: 33 us
  Pallas kernels  32.3 us (98%)
  between operations  0.64 us (2%)
    pallas_call x1, Pallas kernels, per_device(): pl.pallas_call(functools.partial(kernel, nx, ny), out_shape=(vmem((2, *ce...  31.7 us

profile of v3, /device:TPU:1, one launch (start us, length us, event | category | flops | bytes accessed | tf_op | source)
XLA Modules:
  0.0 33.0 jit_solution(623749948391127350)
XLA Ops:
  0.6 31.7 %shard_map.59 = (f32[2,4,32,128]{3,2,1,0:T(8,128)S(1)}, f32[8,128]{1,0:T(8,128)S(1)}) custom-call(bf16[16,4,32,128]{3,2,1,0:T(8,128)(2,1)} %basis_hbm.1, bf16[4,32,128]{2,1,0:T(8,128)(2,1)} %mob_hbm.1, f32[4,32,128]{2,1,0:T(8,128)} %acc_hbm.1, f32[4,32,128]{2,1,0:T(8,128)} %res_hbm.1), custom_call_target="tpu_custom_call" | custom-call | tf_op jit(solution)/shard_map/pallas_call | solution.py:372
  32.3 0.6 %shard_map.60 = (f32[4,32,128]{2,1,0:T(8,128)}, f32[1,1,16]{2,1,0:T(1,128)}) custom-call(f32[2,4,32,128]{3,2,1,0:T(8,128)S(1)} %get-tuple-element.4.f, f32[8,128]{1,0:T(8,128)S(1)} %get-tuple-element.5.s), custom_call_target="tpu_custom_call" | custom-call | tf_op jit(solution)/shard_map/pallas_call | solution.py:411

commit v4 on v3

--- a/solution.py
+++ b/solution.py
@@ -45,8 +45,8 @@
     gx, gy = lax.axis_index("gx"), lax.axis_index("gy")
     chip, core = gx // 2, lax.rem(gx, 2)
     twin = gx + 1 - 2 * core
-    right, left = gx + 1, gx - 1
-    above, below = gy + 1, gy - 1
+    right, left = lax.rem(gx + 1, nx), lax.rem(gx + nx - 1, nx)
+    above, below = lax.rem(gy + 1, ny), lax.rem(gy + ny - 1, ny)
 
     quarters = [pl.ds(k, K // 4) for k in range(0, K, K // 4)]
     loads = [
@@ -72,11 +72,11 @@
     def signal_x(sem, d):
         @pl.when(gx + d < nx)
         def _():
-            signal(sem, gx + d, gy)
+            signal(sem, lax.rem(gx + d, nx), gy)
 
         @pl.when(gx >= d)
         def _():
-            signal(sem, gx - d, gy)
+            signal(sem, lax.rem(gx + nx - d, nx), gy)
 
     def count_x(d):
         return jnp.where(gx + d < nx, 1, 0) + jnp.where(gx >= d, 1, 0)

time: 33.1 us -> 33.1 us (level)
  no operation moved by 1% of the time
where the time goes in v4:
time: 33.1 us; the launch traced here: 33 us
  Pallas kernels  32.3 us (98%)
  between operations  0.64 us (2%)
    pallas_call x1, Pallas kernels, per_device(): pl.pallas_call(functools.partial(kernel, nx, ny), out_shape=(vmem((2, *ce...  31.7 us

profile of v4, /device:TPU:1, one launch (start us, length us, event | category | flops | bytes accessed | tf_op | source)
XLA Modules:
  0.0 33.0 jit_solution(2570812769912359821)
XLA Ops:
  0.6 31.7 %shard_map.59 = (f32[2,4,32,128]{3,2,1,0:T(8,128)S(1)}, f32[8,128]{1,0:T(8,128)S(1)}) custom-call(bf16[16,4,32,128]{3,2,1,0:T(8,128)(2,1)} %basis_hbm.1, bf16[4,32,128]{2,1,0:T(8,128)(2,1)} %mob_hbm.1, f32[4,32,128]{2,1,0:T(8,128)} %acc_hbm.1, f32[4,32,128]{2,1,0:T(8,128)} %res_hbm.1), custom_call_target="tpu_custom_call" | custom-call | tf_op jit(solution)/shard_map/pallas_call | solution.py:372
  32.3 0.6 %shard_map.60 = (f32[4,32,128]{2,1,0:T(8,128)}, f32[1,1,16]{2,1,0:T(1,128)}) custom-call(f32[2,4,32,128]{3,2,1,0:T(8,128)S(1)} %get-tuple-element.4.f, f32[8,128]{1,0:T(8,128)S(1)} %get-tuple-element.5.s), custom_call_target="tpu_custom_call" | custom-call | tf_op jit(solution)/shard_map/pallas_call | solution.py:411

commit v5 on v4

--- a/solution.py
+++ b/solution.py
@@ -200,8 +200,6 @@
     field[0] = p0
     hear_y(0)
     tell_y(1)
-    hear_x(0)
-    tell_x(1)
     edge_p0 = [p0_east, p0_west, hsend[0, 2], hsend[0, 3]]
 
     arrive(0, has)
@@ -238,6 +236,8 @@
         hsend[1, s] = edge_p1[s]
     second = halo(1)
     each(second, gives, lambda c: c.start())
+    hear_x(0)
+    tell_x(1)
 
     bv, qv = coef[0], coef[1]
     qq = jnp.sum(qv * qv, axis=0, keepdims=True)
@@ -317,7 +317,7 @@
     cx0, cy0 = lax.rem(chip, ring_x), chip // ring_x
 
     def hops(d):
-        return min(d[0], ring_x - d[0]) + min(d[1], ring_y - d[1])
+        return min(d[0], ring_x - d[0]) + min(d[1], ring_y - d[1]) + (d[0] > 1) + (d[1] > 1)
 
     for dx, dy in sorted(
         ((i, j) for i in range(ring_x) for j in range(ring_y) if i + j), key=lambda d: -hops(d)

time: 33.1 us -> 33.1 us (level)
  no operation moved by 1% of the time
where the time goes in v5:
time: 33.1 us; the launch traced here: 33 us
  Pallas kernels  32.3 us (98%)
  between operations  0.64 us (2%)
    pallas_call x1, Pallas kernels, per_device(): pl.pallas_call(functools.partial(kernel, nx, ny), out_shape=(vmem((2, *ce...  31.7 us

profile of v5, /device:TPU:1, one launch (start us, length us, event | category | flops | bytes accessed | tf_op | source)
XLA Modules:
  0.0 33.0 jit_solution(2681526787708317339)
XLA Ops:
  0.6 31.7 %shard_map.59 = (f32[2,4,32,128]{3,2,1,0:T(8,128)S(1)}, f32[8,128]{1,0:T(8,128)S(1)}) custom-call(bf16[16,4,32,128]{3,2,1,0:T(8,128)(2,1)} %basis_hbm.1, bf16[4,32,128]{2,1,0:T(8,128)(2,1)} %mob_hbm.1, f32[4,32,128]{2,1,0:T(8,128)} %acc_hbm.1, f32[4,32,128]{2,1,0:T(8,128)} %res_hbm.1), custom_call_target="tpu_custom_call" | custom-call | tf_op jit(solution)/shard_map/pallas_call | solution.py:372
  32.3 0.6 %shard_map.60 = (f32[4,32,128]{2,1,0:T(8,128)}, f32[1,1,16]{2,1,0:T(1,128)}) custom-call(f32[2,4,32,128]{3,2,1,0:T(8,128)S(1)} %get-tuple-element.4.f, f32[8,128]{1,0:T(8,128)S(1)} %get-tuple-element.5.s), custom_call_target="tpu_custom_call" | custom-call | tf_op jit(solution)/shard_map/pallas_call | solution.py:411
